TPU v7x, 32 devices: a whole 2x2x4 slice. The times are simulated.
32 devices in a mesh: replica: 1, mp: 32 (over z, y, x, core), sub: 1.
Axes of the slice: x: 2, y: 2, z: 4, core: 2. Of those that a mesh axis runs over, the one named last changes fastest.
Arguments:
- hidden: bfloat16 [4, 128, 2, 4096], P(None, ('replica', 'mp'), 'sub'), may hold values from -300 to 300
- norm_gain: bfloat16 [2, 4096], P('sub'), may hold values from 0.5 to 1.5
- head_weight: bfloat16 [2, 4096, 32768], P('sub', None, 'mp'), may hold values from -0.09375 to 0.09375
- base_logits: bfloat16 [4, 128, 32768], P(None, ('replica', 'sub'), 'mp'), may hold values from -60 to 300
- tokens: int32 [4, 128], P(None, ('replica', 'sub')), may hold values from 0 to 32767
- cache_length: int32 [128], P(('replica', 'sub')), may hold values from 1 to 8192
Outputs:
- log_probs: float32 [4, 128, 32768], P(None, ('replica', 'sub'), 'mp')
- chosen: float32 [4, 128], P(None, ('replica', 'sub'))
- ranking: float32 [128], P(('replica', 'sub'))
All inputs are finite; a program needn't handle non-finite values.
Results may differ from a plain program's by a relative error of at most 0.00047.
Values may be sent and summed in bfloat16 or wider, within the bound.
A program may use at most 64 MiB of HBM per device.

v0:
```python
import jax
import jax.numpy as jnp
from jax import lax
from jax.sharding import PartitionSpec as P

ALPHA = 2.0
EPSILON = 1e-05


def score_block(normed, base_block, token_block, weights, slice_start):
    logits = jnp.einsum(
        "srmd,mdv->smrv",
        lax.all_gather(normed, "mp", axis=1, tiled=True),
        weights,
        preferred_element_type=jnp.float32,
    ).astype(jnp.bfloat16)
    step_count, model_count, row_count, vocab_width = logits.shape
    groups = lax.axis_size("sub")
    shares = logits.reshape(step_count, model_count, groups, row_count // groups, vocab_width)
    paired = lax.all_to_all(shares, "sub", split_axis=2, concat_axis=1, tiled=True)
    paired = paired.reshape(step_count, 2, row_count // groups, vocab_width)
    combined = base_block.astype(jnp.float32) + ALPHA * (
        paired[:, 0].astype(jnp.float32) - paired[:, 1].astype(jnp.float32)
    )
    columns = lax.broadcasted_iota(jnp.int32, (1, 1, vocab_width), 2) + slice_start
    picked_part = jnp.sum(jnp.where(columns == token_block[:, :, None], combined, 0.0), axis=2)
    maximum = lax.pmax(jnp.max(combined, axis=2), "mp")
    partial_value = jnp.sum(jnp.exp(combined - maximum[:, :, None]), axis=2)
    summed, picked = lax.psum((partial_value, picked_part), "mp")
    log_summed = jnp.log(summed)
    log_block = combined - maximum[:, :, None] - log_summed[:, :, None]
    chosen_block = picked - maximum - log_summed
    return (log_block, chosen_block)


def on_device(hidden, norm_gain, head_weight, base_logits, tokens, cache_length):
    step_count = hidden.shape[0]
    slice_start = lax.axis_index("mp") * head_weight.shape[2]
    values = hidden.astype(jnp.float32)
    mean_square = jnp.mean(values * values, axis=-1, keepdims=True)
    normed = (
        values * lax.rsqrt(mean_square + EPSILON) * norm_gain.astype(jnp.float32)[None, None]
    ).astype(jnp.bfloat16)
    log_parts = []
    chosen_parts = []
    for moment in range(step_count):
        log_block, chosen_block = score_block(
            normed[moment : moment + 1],
            base_logits[moment : moment + 1],
            tokens[moment : moment + 1],
            head_weight,
            slice_start,
        )
        log_parts.append(log_block)
        chosen_parts.append(chosen_block)
    log_probs = jnp.concatenate(log_parts, axis=0)
    chosen = jnp.concatenate(chosen_parts, axis=0)
    penalty = ((5.0 + cache_length.astype(jnp.float32) + step_count) / 6.0) ** 0.6
    ranking = jnp.sum(chosen, axis=0) / penalty
    return (log_probs, chosen, ranking)


def solution(mesh):
    return jax.shard_map(
        on_device,
        mesh=mesh,
        in_specs=(
            P(None, ("replica", "mp"), "sub", None),
            P("sub", None),
            P("sub", None, "mp"),
            P(None, ("replica", "sub"), "mp"),
            P(None, ("replica", "sub")),
            P(("replica", "sub")),
        ),
        out_specs=(
            P(None, ("replica", "sub"), "mp"),
            P(None, ("replica", "sub")),
            P(("replica", "sub")),
        ),
        check_vma=False,
    )
```

profile of v0, /device:TPU:0, one launch (start us, length us, event | category | flops | bytes accessed | tf_op | source)
XLA Modules:
  0.0 346.7 jit_solution(15949387448017709900)
XLA Ops:
  7.2 0.0 all-gather.11.cloned.1.call-start
  7.2 0.7 convert_element_type.170
  7.9 1.3 fusion.36
  9.3 1.3 fusion.38
  10.6 0.9 fusion.43
  11.5 0.0 all-gather.11.cloned.1.call-update
  11.5 0.0 all-gather.9.cloned.1.call-start
  11.6 0.7 all-gather.9.cloned.1.call-update
  12.3 0.0 all-gather.7.cloned.1.call-start
  12.3 0.7 all-gather.7.cloned.1.call-update
  13.0 0.0 all-gather.5.cloned.1.call-start
  13.0 0.5 all-gather.5.cloned.1.call-update
  13.6 0.8 slice_bitcast_fusion.2
  14.4 56.3 %all-gather.11.cloned.1.call-done = bf16[1,128,2,4096]{3,2,0,1:T(2,128)(2,1)} async-done(((bf16[1,4,2,4096]{3,2,0,1:T(2,128)(2,1)}), bf16[1,128,2,4096]{3,2,0,1:T(2,128)(2,1)}) %all-gather.11.cloned.1.call-update) | async-done | bytes 2097168 | tf_op jit(solution)/shard_map/all_gather | solution.py:13
  70.7 10.7 %fusion.24 = bf16[1,2,128,1024]{3,2,1,0:T(8,128)(2,1)S(1)} fusion(bf16[2,4096,1024]{2,1,0:T(8,128)(2,1)} %param.8, bf16[1,128,2,4096]{3,2,0,1:T(2,128)(2,1)} %all-gather.11.cloned.1.call-done), kind=kOutput, calls=%fused_computation.17 | convolution fusion | flops 2147745792 | bytes 19398656 | tf_op jit(solution)/shard_map/srmd,mdv->smrv/dot_general | solution.py:11
  81.5 47.4 %all-gather.9.cloned.1.call-done = bf16[1,128,2,4096]{3,2,0,1:T(2,128)(2,1)} async-done(((bf16[1,4,2,4096]{3,2,0,1:T(2,128)(2,1)}), bf16[1,128,2,4096]{3,2,0,1:T(2,128)(2,1)}) %all-gather.9.cloned.1.call-update) | async-done | bytes 2097168 | tf_op jit(solution)/shard_map/all_gather | solution.py:13
  128.9 10.7 %fusion.27 = bf16[1,2,128,1024]{3,2,1,0:T(8,128)(2,1)S(1)} fusion(bf16[2,4096,1024]{2,1,0:T(8,128)(2,1)} %param.8, bf16[1,128,2,4096]{3,2,0,1:T(2,128)(2,1)} %all-gather.9.cloned.1.call-done), kind=kOutput, calls=%fused_computation.18 | convolution fusion | flops 2147745792 | bytes 19398656 | tf_op jit(solution)/shard_map/srmd,mdv->smrv/dot_general | solution.py:11
  139.6 47.4 %all-gather.7.cloned.1.call-done = bf16[1,128,2,4096]{3,2,0,1:T(2,128)(2,1)} async-done(((bf16[1,4,2,4096]{3,2,0,1:T(2,128)(2,1)}), bf16[1,128,2,4096]{3,2,0,1:T(2,128)(2,1)}) %all-gather.7.cloned.1.call-update) | async-done | bytes 2097168 | tf_op jit(solution)/shard_map/all_gather | solution.py:13
  187.0 10.9 %fusion.30 = bf16[1,2,128,1024]{3,2,1,0:T(8,128)(2,1)S(1)} fusion(bf16[2,4096,1024]{2,1,0:T(8,128)(2,1)} %param.8, bf16[1,128,2,4096]{3,2,0,1:T(2,128)(2,1)} %all-gather.7.cloned.1.call-done), kind=kOutput, calls=%fused_computation.19 | convolution fusion | flops 2147745792 | bytes 19398656 | tf_op jit(solution)/shard_map/srmd,mdv->smrv/dot_general | solution.py:11
  197.9 47.0 %all-gather.5.cloned.1.call-done = bf16[1,128,2,4096]{3,2,0,1:T(2,128)(2,1)} async-done(((bf16[1,4,2,4096]{3,2,0,1:T(2,128)(2,1)}), bf16[1,128,2,4096]{3,2,0,1:T(2,128)(2,1)}) %all-gather.5.cloned.1.call-update) | async-done | bytes 2097168 | tf_op jit(solution)/shard_map/all_gather | solution.py:13
  245.0 10.8 %fusion.33 = bf16[1,2,128,1024]{3,2,1,0:T(8,128)(2,1)S(1)} fusion(bf16[2,4096,1024]{2,1,0:T(8,128)(2,1)} %param.8, bf16[1,128,2,4096]{3,2,0,1:T(2,128)(2,1)} %all-gather.5.cloned.1.call-done), kind=kOutput, calls=%fused_computation.20 | convolution fusion | flops 2147745792 | bytes 19398656 | tf_op jit(solution)/shard_map/srmd,mdv->smrv/dot_general | solution.py:11
  255.7 0.6 fusion.39
  256.3 38.6 %all-reduce.1 = (f32[1,128]{1,0:T(1,128)S(1)}, f32[1,128]{1,0:T(1,128)S(1)}, f32[1,128]{1,0:T(1,128)S(1)}, f32[1,128]{1,0:T(1,128)S(1)}) all-reduce(f32[1,128]{1,0:T(1,128)S(1)} %bitcast.149, f32[1,128]{1,0:T(1,128)S(1)} %bitcast.148, f32[1,128]{1,0:T(1,128)S(1)} %bitcast.146, ...), channel_id=1, replica_groups=mesh['replica'=1,'mp'=32,'sub'=1] {'mp'}, use_global_device_ids=true, to_apply=%region_10.11 | all-reduce | flops 512 | bytes 4096 | tf_op jit(solution)/shard_map/pmax | solution.py:27
  294.8 0.5 select_reduce_fusion.3
  295.4 0.5 select_reduce_fusion.1
  295.9 40.8 %all-reduce = (f32[1,128]{1,0:T(1,128)S(1)}, f32[1,128]{1,0:T(1,128)S(1)}, f32[1,128]{1,0:T(1,128)S(1)}, f32[1,128]{1,0:T(1,128)S(1)}, f32[1,128]{1,0:T(1,128)S(...) all-reduce(f32[1,128]{1,0:T(1,128)S(1)} %bitcast.144, ...), channel_id=1, replica_groups=mesh['replica'=1,'mp'=32,'sub'=1] {'mp'}, use_global_device_ids=true, to_apply=%region_16.17 | all-reduce | flops 1024 | bytes 8192 | tf_op jit(solution)/shard_map/psum | solution.py:29
  336.7 0.2 subtract_subtract_fusion.2
  336.9 0.4 subtract_subtract_fusion.3
  337.4 0.2 copy-done.1
  337.6 0.5 bitcast_multiply_fusion
  338.1 0.6 pad_maximum_fusion.1
  338.7 1.5 pad_maximum_fusion
  (7 shorter events, 0.0 us)
Async XLA Ops:
  7.2 63.6 %all-gather.11.cloned.1.call-start = ((), (), s32[]{:S(2)}) async-start(), calls=%async_computation.3 | async-start | bytes 2162688 | tf_op jit(solution)/shard_map/all_gather | solution.py:13
  11.5 117.4 %all-gather.9.cloned.1.call-start = ((), (), s32[]{:S(2)}) async-start(), calls=%async_computation.2 | async-start | bytes 2162688 | tf_op jit(solution)/shard_map/all_gather | solution.py:13
  12.3 174.7 %all-gather.7.cloned.1.call-start = ((), (), s32[]{:S(2)}) async-start(), calls=%async_computation.1 | async-start | bytes 2162688 | tf_op jit(solution)/shard_map/all_gather | solution.py:13
  13.0 232.0 %all-gather.5.cloned.1.call-start = ((), (), s32[]{:S(2)}) async-start(), calls=%async_computation | async-start | bytes 2162688 | tf_op jit(solution)/shard_map/all_gather | solution.py:13
  197.9 57.8 %copy-start = (bf16[4,128,1024]{2,1,0:T(8,128)(2,1)S(1)}, bf16[4,128,1024]{2,1,0:T(8,128)(2,1)}, u32[]{:S(2)}) copy-start(bf16[4,128,1024]{2,1,0:T(8,128)(2,1)} %param.9) | copy-start | bytes 3145732
  336.9 0.7 copy-start.1
Sparse Core Ops, SparseCore 0:
  11.6 59.0 all-gather.10
  73.6 55.2 all-gather.8
  131.7 55.2 all-gather.6
  189.7 55.2 all-gather.4
where the time goes:
time: 347 us
  waiting for transfers between devices  200 us (58%)
  blocking collectives  79.4 us (23%)
  matrix products  43.1 us (12%)
  between operations  13.9 us (4%)
  other arithmetic  8.18 us (2%)
    all_gather x4, waiting for transfers between devices, score_block(): lax.all_gather(normed, 'mp', axis=1, tiled=True)  198 us
    dot_general x4, matrix products, score_block(): jnp.einsum('srmd,mdv->smrv', lax.all_gather(normed, 'mp', axis=1, tiled=T...  43.1 us
    psum x1, blocking collectives, score_block(): summed, picked = lax.psum((partial_value, picked_part), 'mp')  40.8 us
    pmax x1, blocking collectives, score_block(): maximum = lax.pmax(jnp.max(combined, axis=2), 'mp')  38.6 us
  transfers between devices with their start and end apart: 4, of which 4 were waited for; matrix products, arithmetic and copies ran while one was open for 10% of the time, Pallas kernels for 0%

commit v1 on v0

--- a/solution.py
+++ b/solution.py
@@ -1,6 +1,10 @@
+import functools
+
 import jax
 import jax.numpy as jnp
 from jax import lax
+from jax.experimental import pallas as pl
+from jax.experimental.pallas import tpu as pltpu
 from jax.sharding import PartitionSpec as P
 
 ALPHA = 2.0
@@ -59,10 +63,364 @@
     ranking = jnp.sum(chosen, axis=0) / penalty
     return (log_probs, chosen, ranking)
 
+CHUNKS = 8
+AHEAD = 2
+PLANE = 4
+DEPTH = 4
+CORES = 2
+
+
+def remote(source, target, send_sem, recv_sem, device):
+    return pltpu.make_async_remote_copy(
+        src_ref=source,
+        dst_ref=target,
+        send_sem=send_sem,
+        recv_sem=recv_sem,
+        device_id={"mp": device},
+        device_id_type=pl.DeviceIdType.MESH,
+    )
+
+
+def expert_kernel(
+    normed,
+    weight_hbm,
+    base_hbm,
+    tokens,
+    cache_length,
+    out,
+    chosen_out,
+    ranking_out,
+    gathered,
+    weight,
+    acc,
+    base,
+    token_columns,
+    stats,
+    line_stats,
+    plane_stats,
+    weight_sem,
+    base_sem,
+    z_send,
+    z_recv,
+    x_send,
+    x_recv,
+    y_send,
+    y_recv,
+    dx_send,
+    dx_recv,
+    dy_send,
+    dy_recv,
+    s_send,
+    s_recv,
+    line_send,
+    line_recv,
+    plane_send,
+    plane_recv,
+):
+    me = lax.axis_index("mp")
+    z = me // 8
+    q = (me // 2) % 4
+    c = me % 2
+    qx = q + 1 - 2 * (q % 2)
+    qy = (q + 2) % 4
+    qd = qx + 2 - 4 * (qx // 2)
+
+    def device(zz, qq, cc):
+        return zz * 8 + qq * 2 + cc
+
+    x_device = device(z, qx, c)
+    y_device = device(z, qy, c)
+    sibling = device(z, q, 1 - c)
+    blocks = CHUNKS // 2
+    width = normed.shape[2]
+
+    def weight_copy(chunk):
+        return pltpu.make_async_copy(
+            weight_hbm.at[chunk // blocks, pl.ds((chunk % blocks) * width, width), :],
+            weight.at[chunk],
+            weight_sem.at[chunk],
+        )
+
+    base_copy = pltpu.make_async_copy(base_hbm, base, base_sem)
+
+    def z_copy(chunk, shift):
+        peer = (z + shift) % DEPTH
+        return remote(
+            normed.at[chunk], gathered.at[chunk, q, c, z], z_send.at[chunk, peer], z_recv.at[chunk, z], device(peer, q, c)
+        )
+
+    def z_arrival(chunk, shift):
+        peer = (z + shift) % DEPTH
+        return remote(
+            normed.at[chunk], gathered.at[chunk, q, c, peer], z_send.at[chunk, peer], z_recv.at[chunk, peer], device(peer, q, c)
+        )
+
+    def block_copy(chunk, block, send_sem, recv_sem, target):
+        place = gathered.at[chunk, block, c]
+        return remote(place, place, send_sem.at[chunk], recv_sem.at[chunk], target)
+
+    def half_copy(chunk, block, start, send_sem, recv_sem, target):
+        place = gathered.at[chunk, block, c, pl.ds(start, DEPTH // 2)]
+        return remote(place, place, send_sem.at[chunk], recv_sem.at[chunk], target)
+
+    def sibling_copy(chunk, block, core):
+        place = gathered.at[chunk, block, core]
+        return remote(place, place, s_send.at[chunk, block], s_recv.at[chunk, block], sibling)
+
+    barrier = pltpu.get_barrier_semaphore()
+    for shift in range(1, DEPTH):
+        pl.semaphore_signal(barrier, inc=1, device_id={"mp": device((z + shift) % DEPTH, q, c)}, device_id_type=pl.DeviceIdType.MESH)
+    for shift in range(1, PLANE * CORES):
+        other = (me % 8 + shift) % 8
+        pl.semaphore_signal(barrier, inc=1, device_id={"mp": z * 8 + other}, device_id_type=pl.DeviceIdType.MESH)
+
+    @pl.loop(0, CHUNKS)
+    def _(chunk):
+        weight_copy(chunk).start()
+
+    base_copy.start()
+    pl.semaphore_wait(barrier, DEPTH - 1 + PLANE * CORES - 1)
+    for chunk in range(AHEAD):
+        for shift in range(1, DEPTH):
+            z_copy(chunk, shift).start()
+
+    @pl.loop(0, CHUNKS)
+    def _(chunk):
+        gathered[chunk, q, c, z] = normed[chunk]
+
+    steps, rows, columns = out.shape
+    diagonal = lax.broadcasted_iota(jnp.int32, (rows, rows), 0) == lax.broadcasted_iota(jnp.int32, (rows, rows), 1)
+
+    def to_column(line):
+        return jnp.sum(jnp.where(diagonal, jnp.broadcast_to(line, (rows, rows)), 0.0), axis=1, keepdims=True)
+
+    def to_line(square):
+        return jnp.sum(jnp.where(diagonal, square, 0.0), axis=0, keepdims=True)
+
+    for step in range(steps):
+        token_columns[step] = jnp.broadcast_to(to_column(tokens[step : step + 1, :].astype(jnp.float32)), (rows, rows))
+
+    @pl.loop(0, CHUNKS + 3)
+    def _(tick):
+        @pl.when(tick < CHUNKS)
+        def _():
+            chunk = tick
+            for shift in range(1, DEPTH):
+                z_arrival(chunk, shift).wait_recv()
+            block_copy(chunk, q, x_send, x_recv, x_device).start()
+            block_copy(chunk, q, y_send, y_recv, y_device).start()
+            sibling_copy(chunk, q, c).start()
+
+        @pl.when(tick < CHUNKS - AHEAD)
+        def _():
+            for shift in range(1, DEPTH):
+                z_copy(tick + AHEAD, shift).start()
+
+        @pl.when(jnp.logical_and(tick >= 1, tick < CHUNKS + 1))
+        def _():
+            chunk = tick - 1
+            block_copy(chunk, qx, x_send, x_recv, x_device).wait_recv()
+            half_copy(chunk, qx, 0, dy_send, dy_recv, y_device).start()
+            block_copy(chunk, qy, y_send, y_recv, y_device).wait_recv()
+            half_copy(chunk, qy, DEPTH // 2, dx_send, dx_recv, x_device).start()
+            sibling_copy(chunk, qx, c).start()
+            sibling_copy(chunk, qy, c).start()
+
+        @pl.when(jnp.logical_and(tick >= 2, tick < CHUNKS + 2))
+        def _():
+            chunk = tick - 2
+            half_copy(chunk, qd, 0, dy_send, dy_recv, y_device).wait_recv()
+            half_copy(chunk, qd, DEPTH // 2, dx_send, dx_recv, x_device).wait_recv()
+            sibling_copy(chunk, qd, c).start()
+
+        @pl.when(tick >= 3)
+        def _():
+            chunk = tick - 3
+            for block in range(PLANE):
+                sibling_copy(chunk, block, 1 - c).wait_recv()
+            weight_copy(chunk).wait()
+            model = chunk // blocks
+            part = chunk % blocks
+            count = gathered.shape[1] * gathered.shape[2] * gathered.shape[3] * gathered.shape[4]
+            left = gathered[chunk].reshape(count, width)
+
+            @pl.loop(0, columns // 256)
+            def _(tile):
+                at = pl.ds(pl.multiple_of(tile * 256, 256), 256)
+                product = jnp.dot(left, weight[chunk, :, at], preferred_element_type=jnp.float32)
+
+                @pl.when(part == 0)
+                def _():
+                    acc[model, :, at] = product
+
+                @pl.when(part > 0)
+                def _():
+                    acc[model, :, at] += product
+
+    base_copy.wait()
+    slice_start = me * columns
+    column = (lax.broadcasted_iota(jnp.int32, (16, columns), 1) + slice_start).astype(jnp.float32)
+    low = lax.broadcasted_iota(jnp.int32, (8, columns), 0) < 4
+
+    @pl.loop(0, rows // 16)
+    def _(group):
+        zz = group // 2
+        pair = group % 2
+        first = pl.multiple_of(group * 16, 16)
+        parts = [[] for _ in range(steps)]
+        for block in range(2):
+            for tile in range(steps // 2):
+                values = []
+                for core in range(CORES):
+                    place = pl.multiple_of((((pair * 2 + block) * CORES + core) * DEPTH + zz) * 16 + tile * 8, 8)
+                    expert = acc[0, pl.ds(place, 8), :].astype(jnp.bfloat16).astype(jnp.float32)
+                    anti = acc[1, pl.ds(place, 8), :].astype(jnp.bfloat16).astype(jnp.float32)
+                    values.append(ALPHA * (expert - anti))
+                parts[2 * tile].append(jnp.where(low, values[0], pltpu.roll(values[1], 4, 0)))
+                parts[2 * tile + 1].append(jnp.where(low, pltpu.roll(values[0], 4, 0), values[1]))
+        for step in range(steps):
+            combined = base[step, pl.ds(first, 16), :].astype(jnp.float32) + jnp.concatenate(parts[step], axis=0)
+            out[step, pl.ds(first, 16), :] = combined
+            peak = jnp.max(combined, axis=1, keepdims=True)
+            total = jnp.sum(jnp.exp(combined - peak), axis=1, keepdims=True)
+            token = token_columns[step, pl.ds(first, 16), :][:, 0:1]
+            picked = jnp.sum(jnp.where(column == token, combined, 0.0), axis=1, keepdims=True)
+            stats[0, step, pl.ds(first, 16), :] = jnp.broadcast_to(peak, (16, rows))
+            stats[1, step, pl.ds(first, 16), :] = jnp.broadcast_to(total, (16, rows))
+            stats[2, step, pl.ds(first, 16), :] = jnp.broadcast_to(picked, (16, rows))
+
+    for kind in range(3):
+        for step in range(steps):
+            line_stats[z, pl.ds(kind * steps + step, 1), :] = to_line(stats[kind, step])
+
+    def line_copy(shift):
+        peer = (z + shift) % DEPTH
+        return remote(line_stats.at[z], line_stats.at[z], line_send.at[peer], line_recv.at[z], device(peer, q, c))
+
+    def line_arrival(shift):
+        peer = (z + shift) % DEPTH
+        return remote(line_stats.at[peer], line_stats.at[peer], line_send.at[peer], line_recv.at[peer], device(peer, q, c))
+
+    spot = me % 8
+
+    def plane_copy(shift):
+        peer = (spot + shift) % 8
+        return remote(plane_stats.at[spot], plane_stats.at[spot], plane_send.at[peer], plane_recv.at[spot], z * 8 + peer)
+
+    def plane_arrival(shift):
+        peer = (spot + shift) % 8
+        return remote(plane_stats.at[peer], plane_stats.at[peer], plane_send.at[peer], plane_recv.at[peer], z * 8 + peer)
+
+    def merge(ref, count):
+        peaks = [ref[index, 0:steps, :] for index in range(count)]
+        peak = functools.reduce(jnp.maximum, peaks)
+        total = sum(ref[index, steps : 2 * steps, :] * jnp.exp(peaks[index] - peak) for index in range(count))
+        picked = sum(ref[index, 2 * steps : 3 * steps, :] for index in range(count))
+        return peak, total, picked
+
+    for shift in range(1, DEPTH):
+        line_copy(shift).start()
+    for shift in range(1, DEPTH):
+        line_arrival(shift).wait_recv()
+    for index, value in enumerate(merge(line_stats, DEPTH)):
+        plane_stats[spot, pl.ds(index * steps, steps), :] = value
+    for shift in range(1, 8):
+        plane_copy(shift).start()
+    for shift in range(1, 8):
+        plane_arrival(shift).wait_recv()
+    peak, total, picked = merge(plane_stats, 8)
+    log_total = jnp.log(total)
+    chosen = (picked - peak) - log_total
+    chosen_out[...] = chosen
+    penalty = jnp.exp(0.6 * jnp.log((5.0 + cache_length[...].astype(jnp.float32) + steps) / 6.0))
+    ranking_out[...] = jnp.sum(chosen, axis=0, keepdims=True) / penalty
+    for step in range(steps):
+        peak_column = to_column(peak[step : step + 1, :])
+        log_column = to_column(log_total[step : step + 1, :])
+        out[step] = (out[step] - peak_column) - log_column
+
+    for shift in range(1, DEPTH):
+        line_copy(shift).wait_send()
+    for shift in range(1, 8):
+        plane_copy(shift).wait_send()
+
+    @pl.loop(0, CHUNKS)
+    def _(chunk):
+        for shift in range(1, DEPTH):
+            z_copy(chunk, shift).wait_send()
+        block_copy(chunk, q, x_send, x_recv, x_device).wait_send()
+        block_copy(chunk, q, y_send, y_recv, y_device).wait_send()
+        half_copy(chunk, qx, 0, dy_send, dy_recv, y_device).wait_send()
+        half_copy(chunk, qy, DEPTH // 2, dx_send, dx_recv, x_device).wait_send()
+        for block in range(PLANE):
+            sibling_copy(chunk, block, c).wait_send()
+
+
+def on_box(hidden, norm_gain, head_weight, base_logits, tokens, cache_length):
+    steps, own, models, features = hidden.shape
+    rows, columns = base_logits.shape[1:]
+    values = hidden.astype(jnp.float32)
+    mean_square = jnp.mean(values * values, axis=-1, keepdims=True)
+    normed = (
+        values * lax.rsqrt(mean_square + EPSILON) * norm_gain.astype(jnp.float32)[None, None]
+    ).astype(jnp.bfloat16)
+    width = features * models // CHUNKS
+    normed = normed.reshape(steps * own, models * features // width, width).transpose(1, 0, 2)
+    any_space = pl.BlockSpec(memory_space=pl.ANY)
+    local = pl.BlockSpec(memory_space=pltpu.VMEM)
+    chunk_sems = pltpu.SemaphoreType.DMA((CHUNKS,))
+    log_probs, chosen, ranking = pl.pallas_call(
+        expert_kernel,
+        out_shape=(
+            jax.ShapeDtypeStruct((steps, rows, columns), jnp.float32),
+            jax.ShapeDtypeStruct((steps, rows), jnp.float32),
+            jax.ShapeDtypeStruct((1, rows), jnp.float32),
+        ),
+        in_specs=[local, any_space, any_space, local, local],
+        out_specs=(local, local, local),
+        scratch_shapes=[
+            pltpu.VMEM((CHUNKS, PLANE, CORES, DEPTH, steps * own, width), jnp.bfloat16),
+            pltpu.VMEM((CHUNKS, width, columns), jnp.bfloat16),
+            pltpu.VMEM((models, steps * rows, columns), jnp.float32),
+            pltpu.VMEM((steps, rows, columns), jnp.bfloat16),
+            pltpu.VMEM((steps, rows, rows), jnp.float32),
+            pltpu.VMEM((3, steps, rows, rows), jnp.float32),
+            pltpu.VMEM((DEPTH, 3 * steps, rows), jnp.float32),
+            pltpu.VMEM((PLANE * CORES, 3 * steps, rows), jnp.float32),
+            chunk_sems,
+            pltpu.SemaphoreType.DMA,
+            pltpu.SemaphoreType.DMA((CHUNKS, DEPTH)),
+            pltpu.SemaphoreType.DMA((CHUNKS, DEPTH)),
+            chunk_sems,
+            chunk_sems,
+            chunk_sems,
+            chunk_sems,
+            chunk_sems,
+            chunk_sems,
+            chunk_sems,
+            chunk_sems,
+            pltpu.SemaphoreType.DMA((CHUNKS, PLANE)),
+            pltpu.SemaphoreType.DMA((CHUNKS, PLANE)),
+            pltpu.SemaphoreType.DMA((DEPTH,)),
+            pltpu.SemaphoreType.DMA((DEPTH,)),
+            pltpu.SemaphoreType.DMA((PLANE * CORES,)),
+            pltpu.SemaphoreType.DMA((PLANE * CORES,)),
+        ],
+        compiler_params=pltpu.CompilerParams(
+            collective_id=0, has_side_effects=True, vmem_limit_bytes=52 << 20
+        ),
+        name="experts",
+    )(normed, head_weight, base_logits, tokens, cache_length.reshape(1, rows))
+    return (log_probs, chosen, ranking.reshape(rows))
+
+
+def fits_box(mesh):
+    return mesh.shape["replica"] == 1 and mesh.shape["sub"] == 1 and mesh.shape["mp"] == PLANE * DEPTH * CORES
+
 
 def solution(mesh):
     return jax.shard_map(
-        on_device,
+        on_box if fits_box(mesh) else on_device,
         mesh=mesh,
         in_specs=(
             P(None, ("replica", "mp"), "sub", None),

time: 347 us -> 75.8 us (0.22)
  waiting for transfers between devices: 200 us -> 0 us
  blocking collectives: 79.4 us -> 0 us
  Pallas kernels: 0 us -> 65.5 us
  matrix products: 43.1 us -> 0 us
  between operations: 13.9 us -> 0.69 us
  other arithmetic: 8.18 us -> 3.46 us
  local copies, waits for them, and re-layouts: 1.93 us -> 5.8 us
    all_gather x4 -> x0, waiting for transfers between devices: 198 us -> none  [score_block(): lax.all_gather(normed, 'mp', axis=1, tiled=True)]
    pallas_call x0 -> x1, Pallas kernels: none -> 65.5 us  [on_box(): pl.pallas_call(expert_kernel, out_shape=(jax.ShapeDtypeStruct((steps, row...]
    dot_general x4 -> x0, matrix products: 43.1 us -> none  [score_block(): jnp.einsum('srmd,mdv->smrv', lax.all_gather(normed, 'mp', axis=1, tiled=T...]
    psum x1 -> x0, blocking collectives: 40.8 us -> none  [score_block(): summed, picked = lax.psum((partial_value, picked_part), 'mp')]
    pmax x1 -> x0, blocking collectives: 38.6 us -> none  [score_block(): maximum = lax.pmax(jnp.max(combined, axis=2), 'mp')]
    unnamed x4 -> x9, local copies, waits for them, and re-layouts: 0.19 us -> 5.58 us
  transfers between devices with their start and end apart: 4 -> 0, of which waited for: 4 -> 0; matrix products, arithmetic and copies ran while one was open for 10% -> 0% of each run, Pallas kernels for 0% -> 0%
where the time goes in v1:
time: 75.8 us; the launch traced here: 75.5 us
  Pallas kernels  65.5 us (86%)
  local copies, waits for them, and re-layouts  5.8 us (8%)
  other arithmetic  3.46 us (5%)
    pallas_call x1, Pallas kernels, on_box(): pl.pallas_call(expert_kernel, out_shape=(jax.ShapeDtypeStruct((steps, row...  65.5 us
    unnamed x9, local copies, waits for them, and re-layouts  5.58 us

profile of v1, /device:TPU:0, one launch (start us, length us, event | category | flops | bytes accessed | tf_op | source)
XLA Modules:
  0.0 75.5 jit_solution(10392742528471990880)
XLA Ops:
  0.6 0.0 copy-start
  0.6 1.4 %fusion = f32[4,4,2]{2,1,0:T(4,128)S(1)} fusion(bf16[4,4,2,4096]{3,2,1,0:T(2,128)(2,1)} %param.6), kind=kLoop, calls=%fused_computation.2 | loop fusion | flops 393184 | bytes 262272 | tf_op jit(solution)/shard_map/reduce_sum | solution.py:363
  2.1 0.7 convert_element_type.10
  2.8 1.3 %fusion.2 = bf16[4,4,2,4096]{3,2,1,0:T(2,128)(2,1)S(1)} fusion(bf16[4,4,2,4096]{3,2,1,0:T(2,128)(2,1)} %param.6, f32[2,4096]{1,0:T(2,128)S(1)} %convert_element_type.10, f32[4,4,2]{2,1,0:T(4,128)S(1)} %add_rsqrt_fusion), kind=kLoop, calls=%fused_computation.4 | loop fusion | flops 524288 | bytes 557184 | tf_op jit(solution)/shard_map/convert_element_type | solution.py:366
  4.1 0.1 reshape.24
  4.2 0.2 copy.11
  4.3 0.0 copy-done
  4.3 0.0 copy-start.1
  4.4 0.7 copy-done.1
  5.0 0.0 copy-start.2
  5.0 0.7 copy-done.2
  5.7 65.5 %experts.1 = (f32[4,128,1024]{2,1,0:T(8,128)}, f32[4,128]{1,0:T(4,128)S(1)}, f32[1,128]{1,0:T(1,128)S(1)}) custom-call(bf16[8,16,1024]{2,1,0:T(8,128)(2,1)S(1)} %bitcast.5, bf16[2,4096,1024]{2,1,0:T(8,128)(2,1)} %weight_hbm.1, bf16[4,128,1024]{2,1,0:T(8,128)(2,1)S(1)} %copy-done, s32[4,128]{1,0:T(4,128)S(1)} %copy-done.1, s32[1,128]{1,0:T(1,128)S(1)} %bitcast.6), custom_call_target="tpu_custom_call" | custom-call | tf_op jit(solution)/shard_map/experts/pallas_call | solution.py:372
  71.2 3.2 %copy.15 = f32[4,128,1024]{2,1,0:T(8,128)} copy(f32[4,128,1024]{2,1,0:T(8,128)} %get-tuple-element.12) | data formatting | bytes 4194304
  74.4 0.6 copy.16
  75.0 0.5 copy.17
  (1 shorter events, 0.0 us)
Async XLA Ops:
  0.6 3.7 %copy-start = (bf16[4,128,1024]{2,1,0:T(8,128)(2,1)S(1)}, bf16[4,128,1024]{2,1,0:T(8,128)(2,1)}, u32[]{:S(2)}) copy-start(bf16[4,128,1024]{2,1,0:T(8,128)(2,1)} %base_hbm.1) | copy-start | bytes 3145732
  4.3 0.7 copy-start.1
  5.0 0.7 copy-start.2

commit v2 on v1

--- a/solution.py
+++ b/solution.py
@@ -81,15 +81,46 @@
     )
 
 
+def diagonal_of(rows):
+    return lax.broadcasted_iota(jnp.int32, (rows, rows), 0) == lax.broadcasted_iota(jnp.int32, (rows, rows), 1)
+
+
+def to_column(line, diagonal):
+    square = jnp.broadcast_to(line, diagonal.shape)
+    return jnp.sum(jnp.where(diagonal, square, 0.0), axis=1, keepdims=True)
+
+
+def finish_kernel(combined, merged, cache_length, out_hbm, chosen_out, ranking_out, out, out_sem):
+    steps, rows = chosen_out.shape
+    diagonal = diagonal_of(rows)
+    log_total = jnp.log(merged[steps : 2 * steps, :])
+    copies = []
+    for step in range(steps):
+        peak_column = to_column(merged[step : step + 1, :], diagonal)
+        log_column = to_column(log_total[step : step + 1, :], diagonal)
+        out[step] = (combined[step] - peak_column) - log_column
+        copies.append(pltpu.make_async_copy(out.at[step], out_hbm.at[step], out_sem.at[step]))
+        copies[-1].start()
+    chosen = (merged[2 * steps : 3 * steps, :] - merged[0:steps, :]) - log_total
+    chosen_out[...] = chosen
+    penalty = jnp.exp(0.6 * jnp.log((5.0 + cache_length[...].astype(jnp.float32) + steps) / 6.0))
+    ranking_out[...] = jnp.sum(chosen, axis=0, keepdims=True) / penalty
+    for copy in copies:
+        copy.wait()
+
+
 def expert_kernel(
-    normed,
+    hidden_hbm,
+    gain_hbm,
     weight_hbm,
     base_hbm,
+    tokens_hbm,
+    out,
+    merged_out,
+    hidden,
+    gain,
     tokens,
-    cache_length,
-    out,
-    chosen_out,
-    ranking_out,
+    values,
     gathered,
     weight,
     acc,
@@ -98,6 +129,9 @@
     stats,
     line_stats,
     plane_stats,
+    hidden_sem,
+    gain_sem,
+    tokens_sem,
     weight_sem,
     base_sem,
     z_send,
@@ -132,7 +166,12 @@
     y_device = device(z, qy, c)
     sibling = device(z, q, 1 - c)
     blocks = CHUNKS // 2
-    width = normed.shape[2]
+    width = gathered.shape[5]
+    hidden_copy = pltpu.make_async_copy(hidden_hbm, hidden, hidden_sem)
+    gain_copy = pltpu.make_async_copy(gain_hbm, gain, gain_sem)
+    tokens_copy = pltpu.make_async_copy(tokens_hbm, tokens, tokens_sem)
+    hidden_copy.start()
+    gain_copy.start()
 
     def weight_copy(chunk):
         return pltpu.make_async_copy(
@@ -146,13 +185,13 @@
     def z_copy(chunk, shift):
         peer = (z + shift) % DEPTH
         return remote(
-            normed.at[chunk], gathered.at[chunk, q, c, z], z_send.at[chunk, peer], z_recv.at[chunk, z], device(peer, q, c)
+            gathered.at[chunk, q, c, z], gathered.at[chunk, q, c, z], z_send.at[chunk, peer], z_recv.at[chunk, z], device(peer, q, c)
         )
 
     def z_arrival(chunk, shift):
         peer = (z + shift) % DEPTH
         return remote(
-            normed.at[chunk], gathered.at[chunk, q, c, peer], z_send.at[chunk, peer], z_recv.at[chunk, peer], device(peer, q, c)
+            gathered.at[chunk, q, c, peer], gathered.at[chunk, q, c, peer], z_send.at[chunk, peer], z_recv.at[chunk, peer], device(peer, q, c)
         )
 
     def block_copy(chunk, block, send_sem, recv_sem, target):
@@ -179,26 +218,33 @@
         weight_copy(chunk).start()
 
     base_copy.start()
+    tokens_copy.start()
+    hidden_copy.wait()
+    gain_copy.wait()
+    steps, own, models, features = hidden.shape
+    for row in range(steps * own):
+        pair = hidden[row // own, row % own].astype(jnp.float32)
+        for model in range(models):
+            values[model, row : row + 1, :] = pair[model : model + 1, :]
+    for model in range(models):
+        value = values[model]
+        mean_square = jnp.mean(value * value, axis=-1, keepdims=True)
+        scaled = value * lax.rsqrt(mean_square + EPSILON) * gain[model : model + 1, :].astype(jnp.float32)
+        for part in range(blocks):
+            gathered[model * blocks + part, q, c, z] = scaled[:, part * width : (part + 1) * width].astype(jnp.bfloat16)
     pl.semaphore_wait(barrier, DEPTH - 1 + PLANE * CORES - 1)
     for chunk in range(AHEAD):
         for shift in range(1, DEPTH):
             z_copy(chunk, shift).start()
-
-    @pl.loop(0, CHUNKS)
-    def _(chunk):
-        gathered[chunk, q, c, z] = normed[chunk]
-
-    steps, rows, columns = out.shape
-    diagonal = lax.broadcasted_iota(jnp.int32, (rows, rows), 0) == lax.broadcasted_iota(jnp.int32, (rows, rows), 1)
-
-    def to_column(line):
-        return jnp.sum(jnp.where(diagonal, jnp.broadcast_to(line, (rows, rows)), 0.0), axis=1, keepdims=True)
+    tokens_copy.wait()
+    rows, columns = out.shape[1:]
+    diagonal = diagonal_of(rows)
 
     def to_line(square):
         return jnp.sum(jnp.where(diagonal, square, 0.0), axis=0, keepdims=True)
 
     for step in range(steps):
-        token_columns[step] = jnp.broadcast_to(to_column(tokens[step : step + 1, :].astype(jnp.float32)), (rows, rows))
+        token_columns[step] = jnp.broadcast_to(to_column(tokens[step : step + 1, :].astype(jnp.float32), diagonal), (rows, rows))
 
     @pl.loop(0, CHUNKS + 3)
     def _(tick):
@@ -328,16 +374,8 @@
         plane_copy(shift).start()
     for shift in range(1, 8):
         plane_arrival(shift).wait_recv()
-    peak, total, picked = merge(plane_stats, 8)
-    log_total = jnp.log(total)
-    chosen = (picked - peak) - log_total
-    chosen_out[...] = chosen
-    penalty = jnp.exp(0.6 * jnp.log((5.0 + cache_length[...].astype(jnp.float32) + steps) / 6.0))
-    ranking_out[...] = jnp.sum(chosen, axis=0, keepdims=True) / penalty
-    for step in range(steps):
-        peak_column = to_column(peak[step : step + 1, :])
-        log_column = to_column(log_total[step : step + 1, :])
-        out[step] = (out[step] - peak_column) - log_column
+    for index, value in enumerate(merge(plane_stats, 8)):
+        merged_out[index * steps : (index + 1) * steps, :] = value
 
     for shift in range(1, DEPTH):
         line_copy(shift).wait_send()
@@ -359,26 +397,27 @@
 def on_box(hidden, norm_gain, head_weight, base_logits, tokens, cache_length):
     steps, own, models, features = hidden.shape
     rows, columns = base_logits.shape[1:]
-    values = hidden.astype(jnp.float32)
-    mean_square = jnp.mean(values * values, axis=-1, keepdims=True)
-    normed = (
-        values * lax.rsqrt(mean_square + EPSILON) * norm_gain.astype(jnp.float32)[None, None]
-    ).astype(jnp.bfloat16)
     width = features * models // CHUNKS
-    normed = normed.reshape(steps * own, models * features // width, width).transpose(1, 0, 2)
-    any_space = pl.BlockSpec(memory_space=pl.ANY)
+    far = pl.BlockSpec(memory_space=pltpu.HBM)
     local = pl.BlockSpec(memory_space=pltpu.VMEM)
     chunk_sems = pltpu.SemaphoreType.DMA((CHUNKS,))
-    log_probs, chosen, ranking = pl.pallas_call(
+    line_sems = pltpu.SemaphoreType.DMA((DEPTH,))
+    plane_sems = pltpu.SemaphoreType.DMA((PLANE * CORES,))
+    each_sems = pltpu.SemaphoreType.DMA((CHUNKS, DEPTH))
+    one_sem = pltpu.SemaphoreType.DMA
+    combined, merged = pl.pallas_call(
         expert_kernel,
         out_shape=(
             jax.ShapeDtypeStruct((steps, rows, columns), jnp.float32),
-            jax.ShapeDtypeStruct((steps, rows), jnp.float32),
-            jax.ShapeDtypeStruct((1, rows), jnp.float32),
+            jax.ShapeDtypeStruct((3 * steps, rows), jnp.float32),
         ),
-        in_specs=[local, any_space, any_space, local, local],
-        out_specs=(local, local, local),
+        in_specs=[far] * 5,
+        out_specs=(local, local),
         scratch_shapes=[
+            pltpu.VMEM(hidden.shape, jnp.bfloat16),
+            pltpu.VMEM(norm_gain.shape, jnp.bfloat16),
+            pltpu.VMEM(tokens.shape, jnp.int32),
+            pltpu.VMEM((models, steps * own, features), jnp.float32),
             pltpu.VMEM((CHUNKS, PLANE, CORES, DEPTH, steps * own, width), jnp.bfloat16),
             pltpu.VMEM((CHUNKS, width, columns), jnp.bfloat16),
             pltpu.VMEM((models, steps * rows, columns), jnp.float32),
@@ -387,30 +426,38 @@
             pltpu.VMEM((3, steps, rows, rows), jnp.float32),
             pltpu.VMEM((DEPTH, 3 * steps, rows), jnp.float32),
             pltpu.VMEM((PLANE * CORES, 3 * steps, rows), jnp.float32),
+            one_sem,
+            one_sem,
+            one_sem,
             chunk_sems,
-            pltpu.SemaphoreType.DMA,
-            pltpu.SemaphoreType.DMA((CHUNKS, DEPTH)),
-            pltpu.SemaphoreType.DMA((CHUNKS, DEPTH)),
-            chunk_sems,
-            chunk_sems,
-            chunk_sems,
-            chunk_sems,
-            chunk_sems,
-            chunk_sems,
-            chunk_sems,
-            chunk_sems,
-            pltpu.SemaphoreType.DMA((CHUNKS, PLANE)),
-            pltpu.SemaphoreType.DMA((CHUNKS, PLANE)),
-            pltpu.SemaphoreType.DMA((DEPTH,)),
-            pltpu.SemaphoreType.DMA((DEPTH,)),
-            pltpu.SemaphoreType.DMA((PLANE * CORES,)),
-            pltpu.SemaphoreType.DMA((PLANE * CORES,)),
-        ],
+            one_sem,
+        ]
+        + [each_sems] * 2
+        + [chunk_sems] * 8
+        + [each_sems] * 2
+        + [line_sems] * 2
+        + [plane_sems] * 2,
         compiler_params=pltpu.CompilerParams(
-            collective_id=0, has_side_effects=True, vmem_limit_bytes=52 << 20
+            collective_id=0, has_side_effects=True, vmem_limit_bytes=40 << 20
         ),
         name="experts",
-    )(normed, head_weight, base_logits, tokens, cache_length.reshape(1, rows))
+    )(*[pltpu.with_memory_space_constraint(value, pltpu.HBM) for value in (hidden, norm_gain, head_weight, base_logits, tokens)])
+    log_probs, chosen, ranking = pl.pallas_call(
+        finish_kernel,
+        out_shape=(
+            jax.ShapeDtypeStruct((steps, rows, columns), jnp.float32),
+            jax.ShapeDtypeStruct((steps, rows), jnp.float32),
+            jax.ShapeDtypeStruct((1, rows), jnp.float32),
+        ),
+        in_specs=[local] * 3,
+        out_specs=(far, local, local),
+        scratch_shapes=[
+            pltpu.VMEM((steps, rows, columns), jnp.float32),
+            pltpu.SemaphoreType.DMA((steps,)),
+        ],
+        compiler_params=pltpu.CompilerParams(vmem_limit_bytes=16 << 20),
+        name="finish",
+    )(combined, merged, cache_length.reshape(1, rows))
     return (log_probs, chosen, ranking.reshape(rows))
 
 

time: 75.8 us -> 66.8 us (0.88)
  local copies, waits for them, and re-layouts: 5.8 us -> 0.01 us
  other arithmetic: 3.46 us -> 0 us
    unnamed x9 -> x2, local copies, waits for them, and re-layouts: 5.58 us -> 0.01 us
    pallas_call x0 -> x1, Pallas kernels: none -> 2.06 us  [on_box(): pl.pallas_call(finish_kernel, out_shape=(jax.ShapeDtypeStruct((steps, row...]
    convert_element_type x2 -> x0, other arithmetic: 2.05 us -> none  [the longest x1 1.31 us: on_box(): normed = (values * lax.rsqrt(mean_square + EPSILON) * norm_gain.astype(jn...]
    pallas_call x1, Pallas kernels: 65.5 us -> 63.9 us  [on_box(): pl.pallas_call(expert_kernel, out_shape=(jax.ShapeDtypeStruct((steps, row...]
    reduce_sum x1 -> x0, other arithmetic: 1.4 us -> none  [on_box(): mean_square = jnp.mean(values * values, axis=-1, keepdims=True)]
where the time goes in v2:
time: 66.8 us; the launch traced here: 66.6 us
  Pallas kernels  66 us (99%)
    pallas_call x1, Pallas kernels, on_box(): pl.pallas_call(expert_kernel, out_shape=(jax.ShapeDtypeStruct((steps, row...  63.9 us
    pallas_call x1, Pallas kernels, on_box(): pl.pallas_call(finish_kernel, out_shape=(jax.ShapeDtypeStruct((steps, row...  2.06 us

profile of v2, /device:TPU:0, one launch (start us, length us, event | category | flops | bytes accessed | tf_op | source)
XLA Modules:
  0.0 66.6 jit_solution(17808066773484948257)
XLA Ops:
  0.6 0.0 copy-start
  0.6 63.9 %experts.1 = (f32[4,128,1024]{2,1,0:T(8,128)S(1)}, f32[12,128]{1,0:T(8,128)S(1)}) custom-call(bf16[4,4,2,4096]{3,2,1,0:T(2,128)(2,1)} %hidden_hbm.1, bf16[2,4096]{1,0:T(2,128)(2,1)} %gain_hbm.1, bf16[2,4096,1024]{2,1,0:T(8,128)(2,1)} %weight_hbm.1, bf16[4,128,1024]{2,1,0:T(8,128)(2,1)} %base_hbm.1, s32[4,128]{1,0:T(4,128)} %tokens_hbm.1), custom_call_target="tpu_custom_call" | custom-call | tf_op jit(solution)/shard_map/experts/pallas_call | solution.py:408
  64.6 0.0 copy-done
  64.6 2.1 %finish.1 = (f32[4,128,1024]{2,1,0:T(8,128)}, f32[4,128]{1,0:T(4,128)}, f32[1,128]{1,0:T(1,128)}) custom-call(f32[4,128,1024]{2,1,0:T(8,128)S(1)} %get-tuple-element.8.combined, f32[12,128]{1,0:T(8,128)S(1)} %get-tuple-element.9.merged, s32[1,128]{1,0:T(1,128)S(1)} %bitcast.2), custom_call_target="tpu_custom_call" | custom-call | tf_op jit(solution)/shard_map/finish/pallas_call | solution.py:445
Async XLA Ops:
  0.6 63.9 %copy-start = (s32[128]{0:T(128)S(1)}, s32[128]{0:T(128)}, u32[]{:S(2)}) copy-start(s32[128]{0:T(128)} %param.11) | copy-start | bytes 1540

commit v3 on v2

--- a/solution.py
+++ b/solution.py
@@ -262,23 +262,6 @@
             for shift in range(1, DEPTH):
                 z_copy(tick + AHEAD, shift).start()
 
-        @pl.when(jnp.logical_and(tick >= 1, tick < CHUNKS + 1))
-        def _():
-            chunk = tick - 1
-            block_copy(chunk, qx, x_send, x_recv, x_device).wait_recv()
-            half_copy(chunk, qx, 0, dy_send, dy_recv, y_device).start()
-            block_copy(chunk, qy, y_send, y_recv, y_device).wait_recv()
-            half_copy(chunk, qy, DEPTH // 2, dx_send, dx_recv, x_device).start()
-            sibling_copy(chunk, qx, c).start()
-            sibling_copy(chunk, qy, c).start()
-
-        @pl.when(jnp.logical_and(tick >= 2, tick < CHUNKS + 2))
-        def _():
-            chunk = tick - 2
-            half_copy(chunk, qd, 0, dy_send, dy_recv, y_device).wait_recv()
-            half_copy(chunk, qd, DEPTH // 2, dx_send, dx_recv, x_device).wait_recv()
-            sibling_copy(chunk, qd, c).start()
-
         @pl.when(tick >= 3)
         def _():
             chunk = tick - 3
@@ -302,6 +285,23 @@
                 @pl.when(part > 0)
                 def _():
                     acc[model, :, at] += product
+
+        @pl.when(jnp.logical_and(tick >= 1, tick < CHUNKS + 1))
+        def _():
+            chunk = tick - 1
+            block_copy(chunk, qx, x_send, x_recv, x_device).wait_recv()
+            half_copy(chunk, qx, 0, dy_send, dy_recv, y_device).start()
+            block_copy(chunk, qy, y_send, y_recv, y_device).wait_recv()
+            half_copy(chunk, qy, DEPTH // 2, dx_send, dx_recv, x_device).start()
+            sibling_copy(chunk, qx, c).start()
+            sibling_copy(chunk, qy, c).start()
+
+        @pl.when(jnp.logical_and(tick >= 2, tick < CHUNKS + 2))
+        def _():
+            chunk = tick - 2
+            half_copy(chunk, qd, 0, dy_send, dy_recv, y_device).wait_recv()
+            half_copy(chunk, qd, DEPTH // 2, dx_send, dx_recv, x_device).wait_recv()
+            sibling_copy(chunk, qd, c).start()
 
     base_copy.wait()
     slice_start = me * columns

time: 66.8 us -> 66.3 us (level)
  no operation moved by 1% of the time
where the time goes in v3:
time: 66.3 us; the launch traced here: 66.1 us
  Pallas kernels  65.5 us (99%)
    pallas_call x1, Pallas kernels, on_box(): pl.pallas_call(expert_kernel, out_shape=(jax.ShapeDtypeStruct((steps, row...  63.4 us
    pallas_call x1, Pallas kernels, on_box(): pl.pallas_call(finish_kernel, out_shape=(jax.ShapeDtypeStruct((steps, row...  2.06 us

profile of v3, /device:TPU:0, one launch (start us, length us, event | category | flops | bytes accessed | tf_op | source)
XLA Modules:
  0.0 66.1 jit_solution(4353360780659755207)
XLA Ops:
  0.6 0.0 copy-start
  0.6 63.4 %experts.1 = (f32[4,128,1024]{2,1,0:T(8,128)S(1)}, f32[12,128]{1,0:T(8,128)S(1)}) custom-call(bf16[4,4,2,4096]{3,2,1,0:T(2,128)(2,1)} %hidden_hbm.1, bf16[2,4096]{1,0:T(2,128)(2,1)} %gain_hbm.1, bf16[2,4096,1024]{2,1,0:T(8,128)(2,1)} %weight_hbm.1, bf16[4,128,1024]{2,1,0:T(8,128)(2,1)} %base_hbm.1, s32[4,128]{1,0:T(4,128)} %tokens_hbm.1), custom_call_target="tpu_custom_call" | custom-call | tf_op jit(solution)/shard_map/experts/pallas_call | solution.py:408
  64.0 0.0 copy-done
  64.0 2.1 %finish.1 = (f32[4,128,1024]{2,1,0:T(8,128)}, f32[4,128]{1,0:T(4,128)}, f32[1,128]{1,0:T(1,128)}) custom-call(f32[4,128,1024]{2,1,0:T(8,128)S(1)} %get-tuple-element.8.combined, f32[12,128]{1,0:T(8,128)S(1)} %get-tuple-element.9.merged, s32[1,128]{1,0:T(1,128)S(1)} %bitcast.2), custom_call_target="tpu_custom_call" | custom-call | tf_op jit(solution)/shard_map/finish/pallas_call | solution.py:445
Async XLA Ops:
  0.6 63.4 %copy-start = (s32[128]{0:T(128)S(1)}, s32[128]{0:T(128)}, u32[]{:S(2)}) copy-start(s32[128]{0:T(128)} %param.11) | copy-start | bytes 1540
